TPU v7x, 32 devices: a whole 2x2x4 slice. The times are simulated.
32 devices in a mesh: dp: 8 (over z, y), tensor: 4 (over x, core).
Axes of the slice: x: 2, y: 2, z: 4, core: 2. Of those that a mesh axis runs over, the one named last changes fastest.
Arguments:
- query_act: bfloat16 [8, 1024, 1024], P('dp', None, 'tensor'), may hold values from -6 to 6
- rotated_keys: bfloat16 [8, 1024, 256], P('dp'), may hold values from -6 to 6
- value_input: bfloat16 [8, 1024, 256], P('dp'), may hold values from -6 to 6
- grad_out: bfloat16 [8, 1024, 8192], P('dp', 'tensor'), may hold values from -6 to 6
- out_weight: bfloat16 [1024, 8192], P('tensor', 'dp'), may hold values from -0.1875 to 0.1875
- doc_lengths: int32 [8, 4], P('dp'), may hold values from 1 to 512, 1024 in all within a row
Outputs:
- query_grad: bfloat16 [8, 1024, 1024], P('dp', None, 'tensor')
- key_gradient: bfloat16 [8, 4, 512, 128], P('dp', 'tensor')
- value_gradient: bfloat16 [8, 4, 512, 128], P('dp', 'tensor')
- weight_grad: float32 [1024, 8192], P('tensor', 'dp')
All inputs are finite; a program needn't handle non-finite values.
Results may differ from a plain program's by a relative error of at most 0.015.
The roundings to bfloat16 on the way count: a program that leaves them out, or rounds other values in their place, can miss the bound.
Values may be sent and summed in bfloat16 or wider, within the bound.
A program may use at most 128 MiB of HBM per device.

v0:
```python
import jax
import jax.numpy as jnp
from jax import lax
from jax.sharding import PartitionSpec as P

HEAD_SIZE = 128


def swapped(value, axis, apart):
    mask = 2**apart
    pairs = [(source, source ^ mask) for source in range(lax.axis_size(axis))]
    return lax.ppermute(value, axis, pairs)


def shards(query_act, rotated_keys, value_input, grad_out, out_weight, doc_lengths):
    score_scale = HEAD_SIZE ** (-0.5)
    tensor_index = lax.axis_index("tensor")
    kv_group = tensor_index // 2
    own_half = tensor_index % 2
    seq_len = query_act.shape[1]
    head_count = query_act.shape[2] // HEAD_SIZE
    query_heads = query_act[0].reshape(seq_len, head_count, HEAD_SIZE).transpose(1, 0, 2)
    key_rows = lax.dynamic_slice_in_dim(rotated_keys[0], kv_group * HEAD_SIZE, HEAD_SIZE, 1)
    value_rows = lax.dynamic_slice_in_dim(value_input[0], kv_group * HEAD_SIZE, HEAD_SIZE, 1)
    doc_ends = jnp.cumsum(doc_lengths[0])
    positions = jnp.arange(seq_len, dtype=jnp.int32)
    doc_ids = jnp.sum((positions[:, None] >= doc_ends[None, :]).astype(jnp.int32), axis=1)
    block_rows = min(512, seq_len)
    block_count = seq_len // block_rows
    full_weight = lax.all_gather(out_weight, "dp", axis=1, tiled=True)

    def key_reach():
        return seq_len

    def masked_scores(block_idx, key_span):
        first = block_idx * block_rows
        query_block = query_heads[:, first : first + block_rows]
        scores = (
            jnp.einsum("hqd,kd->hqk", query_block, key_rows, preferred_element_type=jnp.float32)
            * score_scale
        )
        allowed = (positions[None, :key_span] <= positions[first : first + block_rows, None]) & (
            doc_ids[None, :key_span] == doc_ids[first : first + block_rows, None]
        )
        return jnp.where(allowed[None], scores, -jnp.inf)

    totals_list = []
    outputs_list = []
    for block_idx in range(block_count):
        key_span = key_reach()
        scores = masked_scores(block_idx, key_span)
        row_max = jnp.max(scores, axis=-1, keepdims=True)
        log_total = row_max + jnp.log(jnp.sum(jnp.exp(scores - row_max), axis=-1, keepdims=True))
        prob_bf16 = jnp.exp(scores - log_total).astype(jnp.bfloat16)
        outputs_list.append(
            jnp.einsum(
                "hqk,kd->hqd", prob_bf16, value_rows, preferred_element_type=jnp.float32
            ).astype(jnp.bfloat16)
        )
        totals_list.append(log_total)
    attn_out = jnp.concatenate(outputs_list, axis=1)
    out_flat = attn_out.transpose(1, 0, 2).reshape(seq_len, head_count * HEAD_SIZE)
    local_rows = grad_out[0]
    gathered = lax.all_gather(local_rows, "tensor", axis=0, tiled=True)
    out_grad = jnp.einsum(
        "sd,hd->sh", gathered, full_weight, preferred_element_type=jnp.float32
    ).astype(jnp.bfloat16)
    weight_part = jnp.einsum("sh,sd->hd", out_flat, gathered, preferred_element_type=jnp.float32)
    weight_grad = lax.psum_scatter(weight_part, "dp", scatter_dimension=1, tiled=True)
    grad_heads = out_grad.reshape(seq_len, head_count, HEAD_SIZE).transpose(1, 0, 2)
    key_accum = jnp.zeros((seq_len, HEAD_SIZE), jnp.float32)
    value_accum = jnp.zeros((seq_len, HEAD_SIZE), jnp.float32)
    query_list = []
    for block_idx in range(block_count):
        key_span = key_reach()
        first = block_idx * block_rows
        scores = masked_scores(block_idx, key_span)
        prob_block = jnp.exp(scores - totals_list[block_idx])
        prob_bf16 = prob_block.astype(jnp.bfloat16)
        grad_block = grad_heads[:, first : first + block_rows]
        out_block = attn_out[:, first : first + block_rows]
        query_block = query_heads[:, first : first + block_rows]
        dprobs = jnp.einsum(
            "hqd,kd->hqk", grad_block, value_rows, preferred_element_type=jnp.float32
        )
        row_delta = jnp.sum(
            grad_block.astype(jnp.float32) * out_block.astype(jnp.float32), axis=-1, keepdims=True
        )
        score_gradient = (prob_block * (dprobs - row_delta) * score_scale).astype(jnp.bfloat16)
        query_list.append(
            jnp.einsum(
                "hqk,kd->hqd", score_gradient, key_rows, preferred_element_type=jnp.float32
            ).astype(jnp.bfloat16)
        )
        key_accum = key_accum.at[:key_span].add(
            jnp.einsum(
                "hqk,hqd->kd", score_gradient, query_block, preferred_element_type=jnp.float32
            )
        )
        value_accum = value_accum.at[:key_span].add(
            jnp.einsum("hqk,hqd->kd", prob_bf16, grad_block, preferred_element_type=jnp.float32)
        )
    query_grad = (
        jnp.concatenate(query_list, axis=1)
        .transpose(1, 0, 2)
        .reshape(1, seq_len, head_count * HEAD_SIZE)
    )
    half_rows = seq_len // 2
    other_start = (1 - own_half) * half_rows
    outgoing = (
        lax.dynamic_slice_in_dim(key_accum, other_start, half_rows, 0),
        lax.dynamic_slice_in_dim(value_accum, other_start, half_rows, 0),
    )
    partner = swapped((outgoing[0], outgoing[1]), "tensor", 0)
    key_mine = lax.dynamic_slice_in_dim(key_accum, own_half * half_rows, half_rows, 0) + partner[0]
    value_mine = (
        lax.dynamic_slice_in_dim(value_accum, own_half * half_rows, half_rows, 0) + partner[1]
    )
    key_gradient = key_mine.astype(jnp.bfloat16).reshape(1, 1, half_rows, HEAD_SIZE)
    value_gradient = value_mine.astype(jnp.bfloat16).reshape(1, 1, half_rows, HEAD_SIZE)
    return (query_grad, key_gradient, value_gradient, weight_grad)


def solution(mesh):
    placed = (
        P("dp", None, "tensor"),
        P("dp", None, None),
        P("dp", None, None),
        P("dp", "tensor", None),
        P("tensor", "dp"),
        P("dp", None),
    )
    return jax.shard_map(
        shards,
        mesh=mesh,
        in_specs=placed,
        out_specs=(
            P("dp", None, "tensor"),
            P("dp", "tensor", None, None),
            P("dp", "tensor", None, None),
            P("tensor", "dp"),
        ),
        check_vma=False,
    )
```

profile of v0, /device:TPU:1, one launch (start us, length us, event | category | flops | bytes accessed | tf_op | source)
XLA Modules:
  0.0 373.7 jit_solution(8681585686457070649)
XLA Ops:
  7.2 0.0 copy-start
  7.2 0.0 copy-start.10
  7.2 0.0 copy-start.5
  7.2 0.0 copy-start.8
  7.2 0.0 all-gather.4.cloned.1.call-start
  7.3 0.7 all-gather.4.cloned.1.call-update
  7.9 0.0 all-gather.6.cloned.1.call-start
  8.0 0.7 all-gather.6.cloned.1.call-update
  8.7 0.0 reduce-scatter.2.cloned.1.call-start
  8.8 0.0 copy-done.10
  8.8 0.2 reduce-window.8
  9.0 0.0 copy-done.5
  9.0 0.2 copy.29
  9.2 0.3 copy.30
  9.5 0.1 convert_reduce_fusion
  9.6 0.9 fusion.9
  10.5 0.0 copy-done.8
  10.5 0.9 fusion.7
  11.4 0.0 copy-start.1
  11.4 0.9 fusion.6
  12.4 0.0 copy-start.3
  12.4 2.2 exponential_reduce_fusion
  14.5 0.1 copy-done.3
  14.7 0.0 copy-done.1
  14.7 0.0 copy-done
  14.7 1.6 convolution_convert_fusion.1
  16.2 67.6 %all-gather.4.cloned.1.call-done = bf16[256,8192]{1,0:T(8,128)(2,1)} async-done(((bf16[256,1024]{1,0:T(8,128)(2,1)}), bf16[256,8192]{1,0:T(8,128)(2,1)}) %all-gather.4.cloned.1.call-update) | async-done | bytes 4194320 | tf_op jit(solution)/shard_map/all_gather | solution.py:30
  83.9 107.6 %all-gather.6.cloned.1.call-done = bf16[1,1024,8192]{2,1,0:T(8,128)(2,1)} async-done(((bf16[1,256,8192]{2,1,0:T(8,128)(2,1)}), bf16[1,1024,8192]{2,1,0:T(8,128)(2,1)}) %all-gather.6.cloned.1.call-update) | async-done | bytes 16777232 | tf_op jit(solution)/shard_map/all_gather | solution.py:64
  191.5 11.5 %fusion.10 = bf16[1024,256]{0,1:T(8,128)(2,1)S(1)} fusion(bf16[256,8192]{1,0:T(8,128)(2,1)} %all-gather.4.cloned.1.call-done, bf16[1,1024,8192]{2,1,0:T(8,128)(2,1)} %all-gather.6.cloned.1.call-done), kind=kOutput, calls=%fused_computation.20 | convolution fusion | flops 4295229440 | bytes 21495808 | tf_op jit(solution)/shard_map/sd,hd->sh/dot_general | solution.py:65
  203.0 0.3 copy.31
  203.3 0.0 copy-start.6
  203.3 3.8 %multiply_reduce_fusion.1 = (f32[2,512]{1,0:T(2,128)S(1)}, f32[2,512]{1,0:T(2,128)S(1)}, bf16[2,512,128]{2,1,0:T(8,128)(2,1)S(1)}) fusion(bf16[2,1024,128]{2,1,0:T(8,128)(2,1)S(1)} %bitcast.100, bf16[2,512,128]{2,1,0:T(8,128)(2,1)S(1)} %convolution_convert_fusion.1, bf16[1,1024,256]{2,1,0:T(8,128)(2,1)S(1)} %copy-done, s32[]{:T(128)S(6)} %select_n.33, ...), kind=kOutput, calls=%fused_computation.34 | convolution fusion | flops 273807360 | bytes 6041604 | tf_op jit(solution)/shard_map/hqk,kd->hqd/dot_general | solution.py:56
  207.1 0.0 copy-done.6
  207.1 0.2 copy.39
  207.3 12.5 %fusion = f32[256,8192]{1,0:T(8,128)} fusion(bf16[1024,256]{0,1:T(8,128)(2,1)S(1)} %bitcast.93, bf16[1,1024,8192]{2,1,0:T(8,128)(2,1)} %all-gather.6.cloned.1.call-done), kind=kOutput, calls=%fused_computation | convolution fusion | flops 4294967296 | bytes 25690112 | tf_op jit(solution)/shard_map/sh,sd->hd/dot_general | solution.py:68
  219.8 0.0 copy-start.7
  219.8 0.0 reduce-scatter.2.cloned.1.call-update
  219.9 1.0 copy-done.7
  220.9 0.0 copy-start.4
  220.9 4.0 %multiply_convert_fusion = bf16[2,512,1024]{1,2,0:T(8,128)(2,1)S(1)} fusion(f32[1024,2,512]{2,0,1:T(8,128)} %copy-done.1, f32[2,512]{1,0:T(2,128)S(1)} %get-tuple-element.93, f32[2,512]{1,0:T(2,128)S(1)} %log_add_fusion, pred[512,1024]{0,1:T(8,128)(4,1)S(1)} %get-tuple-element.94, bf16[2,1024,128]{2,1,0:T(8,128)(2,1)S(1)} %bitcast.101, ...), kind=kOutput, calls=%fused_computation.6 | convolution fusion | flops 275775488 | bytes 7348228 | tf_op jit(solution)/shard_map/hqd,kd->hqk/dot_general | solution.py:83
  224.8 0.7 convolution_bitcast_fusion.2
  225.5 0.0 copy-done.4
  225.5 0.0 copy-start.9
  225.6 1.7 multiply_convert_fusion.1
  227.3 0.0 copy-start.2
  227.3 0.7 fusion.13
  228.0 0.3 collective-permute-start
  228.4 0.0 copy-done.9
  228.4 0.8 convolution_convert_fusion
  229.1 0.4 copy-done.2
  229.6 1.1 convolution_bitcast_fusion
  230.6 1.3 fusion.14
  231.9 0.8 convolution_convert_fusion.2
  232.7 0.3 collective-permute-start.1
  233.0 0.2 copy.38
  233.2 1.0 copy.40
  234.2 0.0 collective-permute-done
  234.2 0.7 fusion.41
  234.9 0.0 collective-permute-done.1
  234.9 1.6 fusion.42
  236.6 130.6 %reduce-scatter.2.cloned.1.call-done = f32[256,1024]{1,0:T(8,128)} async-done(((f32[256,8192]{1,0:T(8,128)}), f32[256,1024]{1,0:T(8,128)}) %reduce-scatter.2.cloned.1.call-update) | async-done | bytes 1048592 | tf_op jit(solution)/shard_map/reduce_scatter | solution.py:69
  (11 shorter events, 0.2 us)
Async XLA Ops:
  7.2 7.5 %copy-start = (bf16[1,1024,256]{2,1,0:T(8,128)(2,1)S(1)}, bf16[1,1024,256]{2,1,0:T(8,128)(2,1)}, u32[]{:S(2)}) copy-start(bf16[1,1024,256]{2,1,0:T(8,128)(2,1)} %param.24) | copy-start | bytes 1572868
  7.2 1.6 copy-start.10
  7.2 1.8 copy-start.5
  7.2 3.3 copy-start.8
  7.2 76.7 %all-gather.4.cloned.1.call-start = ((), (), s32[]{:S(2)}) async-start(), calls=%async_computation.1 | async-start | bytes 4718592 | tf_op jit(solution)/shard_map/all_gather | solution.py:30
  7.9 183.6 %all-gather.6.cloned.1.call-start = ((), (), s32[]{:S(2)}) async-start(), calls=%async_computation.3 | async-start | bytes 20971520 | tf_op jit(solution)/shard_map/all_gather | solution.py:64
  8.7 358.5 %reduce-scatter.2.cloned.1.call-start = ((), (), s32[]{:S(2)}) async-start(), calls=%async_computation.2 | async-start | bytes 9437184 | tf_op jit(solution)/shard_map/reduce_scatter | solution.py:69
  11.4 3.2 copy-start.1
  12.4 2.3 copy-start.3
  203.3 3.8 %copy-start.6 = (bf16[1024,2,128]{2,0,1:T(8,128)(2,1)}, bf16[1024,2,128]{2,0,1:T(8,128)(2,1)S(1)}, u32[]{:S(2)}) copy-start(bf16[1024,2,128]{2,0,1:T(8,128)(2,1)S(1)} %copy.31) | copy-start | bytes 1572868
  219.8 1.0 copy-start.7
  220.9 4.7 %copy-start.4 = (f32[1024,2,512]{2,0,1:T(8,128)S(1)}, f32[1024,2,512]{2,0,1:T(8,128)}, u32[]{:S(2)}) copy-start(f32[1024,2,512]{2,0,1:T(8,128)} %copy-done.3) | copy-start | bytes 12582916
  225.5 2.8 copy-start.9
  227.3 2.3 copy-start.2
  228.0 6.2 %collective-permute-start = (f32[512,128]{1,0:T(8,128)S(1)}, f32[512,128]{1,0:T(8,128)S(1)}, u32[]{:S(2)}, u32[]{:S(2)}) collective-permute-start(f32[512,128]{1,0:T(8,128)S(1)} %constant_dynamic-slice_fusion.1), channel_id=1, source_target_pairs={{0,1},{1,0},{2,3},{3,2},{4,5},{5,4},{6,7},{7,6},{8,9},{9,8},{10,11... | collective-permute-start | bytes 786440 | tf_op jit(solution)/shard_map/ppermute | solution.py:12
  232.7 2.3 collective-permute-start.1
Sparse Core Ops, SparseCore 0:
  10.2 73.6 all-gather.3
  85.4 106.0 all-gather.5
  220.0 147.1 reduce-scatter.1
where the time goes:
time: 375 us; the launch traced here: 374 us
  waiting for transfers between devices  307 us (82%)
  matrix products  42.1 us (11%)
  between operations  14.1 us (4%)
  other arithmetic  5.72 us (2%)
  local copies, waits for them, and re-layouts  3.81 us (1%)
    reduce_scatter x1, waiting for transfers between devices, shards(): lax.psum_scatter(weight_part, 'dp', scatter_dimension=1, tiled=True)  131 us
    all_gather x1, waiting for transfers between devices, shards(): gathered = lax.all_gather(local_rows, 'tensor', axis=0, tiled=True)  108 us
    all_gather x1, waiting for transfers between devices, shards(): full_weight = lax.all_gather(out_weight, 'dp', axis=1, tiled=True)  67.6 us
    dot_general x1, matrix products, shards(): jnp.einsum('sh,sd->hd', out_flat, gathered, preferred_element_type=jnp.fl...  12.5 us
    dot_general x1, matrix products, shards(): jnp.einsum('sd,hd->sh', gathered, full_weight, preferred_element_type=jnp...  11.5 us
  transfers between devices with their start and end apart: 5, of which 3 were waited for; matrix products, arithmetic and copies ran while one was open for 6% of the time, Pallas kernels for 0%

commit v1 on v0

--- a/solution.py
+++ b/solution.py
@@ -1,9 +1,290 @@
+import functools
+
 import jax
 import jax.numpy as jnp
 from jax import lax
+from jax.experimental import pallas as pl
+from jax.experimental.pallas import tpu as pltpu
 from jax.sharding import PartitionSpec as P
 
 HEAD_SIZE = 128
+
+
+MESH = pl.DeviceIdType.MESH
+
+
+def ring_place(index, count):
+    odd = index % 2
+    return (1 - odd) * (index // 2) + odd * (count - 1 - index // 2)
+
+
+def ring_index(place, count):
+    back = place // (count // 2)
+    return (1 - back) * (2 * place) + back * (2 * (count - 1 - place) + 1)
+
+
+def exchange_kernel(
+    dp_count,
+    tensor_count,
+    grad_ref,
+    weight_ref,
+    out_t_ref,
+    out_grad_ref,
+    weight_grad_ref,
+    grads,
+    weights,
+    sums_out,
+    sums_in,
+    accum,
+    own_sem,
+    own_weight_sem,
+    near_send,
+    near_recv,
+    far_send,
+    far_recv,
+    pass_send,
+    pass_recv,
+    weight_send,
+    weight_recv,
+    sum_send,
+    sum_recv,
+):
+    dp_index = lax.axis_index("dp")
+    tensor_index = lax.axis_index("tensor")
+    chip_count = tensor_count // 2
+    chip, core = tensor_index // 2, tensor_index % 2
+    partner = chip * 2 + 1 - core
+    place = ring_place(dp_index, dp_count)
+    ring = (
+        ring_index((place + 1) % dp_count, dp_count),
+        ring_index((place + dp_count - 1) % dp_count, dp_count),
+    )
+    rows = grad_ref.shape[0]
+    half = weight_ref.shape[1] // 2
+    last = dp_count - 1
+    far_chips = [(chip + away) % chip_count for away in range(1, chip_count)]
+
+    def place_rows(index):
+        return pl.ds(pl.multiple_of(index * rows, rows), rows)
+
+    def columns(side, step):
+        if side == 0:
+            owner = ring_index((place + 2 * dp_count - 1 - step) % dp_count, dp_count)
+        else:
+            owner = ring_index((place + 1 + step) % dp_count, dp_count)
+        return pl.ds(pl.multiple_of(owner * (2 * half) + side * half, half), half)
+
+    def own_copy(side, step):
+        return pltpu.make_async_copy(
+            grad_ref.at[:, columns(side, step)],
+            grads.at[side, step, place_rows(tensor_index)],
+            own_sem.at[side, step],
+        )
+
+    def own_weight(side):
+        return pltpu.make_async_copy(
+            weight_ref.at[:, pl.ds(side * half, half)],
+            weights.at[side, last],
+            own_weight_sem.at[side],
+        )
+
+    def near_copy(side, step):
+        return pltpu.make_async_remote_copy(
+            grad_ref.at[:, columns(side, step)],
+            grads.at[side, step, place_rows(tensor_index)],
+            near_send.at[side, step],
+            near_recv.at[side, step],
+            device_id=(dp_index, partner),
+            device_id_type=MESH,
+        )
+
+    def far_copy(away, side, step):
+        return pltpu.make_async_remote_copy(
+            grad_ref.at[:, columns(side, step)],
+            grads.at[side, step, place_rows(tensor_index)],
+            far_send.at[away, side, step],
+            far_recv.at[away, side, step],
+            device_id=(dp_index, far_chips[away] * 2 + core),
+            device_id_type=MESH,
+        )
+
+    def pass_copy(away, side, step):
+        source = (chip + chip_count - 1 - away) % chip_count * 2 + core
+        block = grads.at[side, step, place_rows(source)]
+        return pltpu.make_async_remote_copy(
+            block,
+            block,
+            pass_send.at[away, side, step],
+            pass_recv.at[away, side, step],
+            device_id=(dp_index, partner),
+            device_id_type=MESH,
+        )
+
+    def weight_copy(side, hop):
+        if isinstance(hop, int) and hop == 0:
+            source = weight_ref.at[:, pl.ds(side * half, half)]
+        else:
+            source = weights.at[side, hop - 1]
+        return pltpu.make_async_remote_copy(
+            source,
+            weights.at[side, hop],
+            weight_send.at[side, hop],
+            weight_recv.at[side, hop],
+            device_id=(ring[side], tensor_index),
+            device_id_type=MESH,
+        )
+
+    def sum_copy(side, step):
+        return pltpu.make_async_remote_copy(
+            sums_out.at[side, step],
+            sums_in.at[side, step],
+            sum_send.at[side, step],
+            sum_recv.at[side, step],
+            device_id=(ring[side], tensor_index),
+            device_id_type=MESH,
+        )
+
+    targets = [(dp_index, partner), (ring[0], tensor_index), (ring[1], tensor_index)]
+    targets += [(dp_index, other * 2 + core) for other in far_chips]
+    barrier = pltpu.get_barrier_semaphore()
+    for target in targets:
+        pl.semaphore_signal(barrier, inc=1, device_id=target, device_id_type=MESH)
+    pl.semaphore_wait(barrier, len(targets))
+
+    for side in (0, 1):
+        weight_copy(side, 0).start()
+        own_weight(side).start()
+
+    @pl.loop(0, dp_count)
+    def _(step):
+        for side in (0, 1):
+            for away in range(chip_count - 1):
+                far_copy(away, side, step).start()
+
+    @pl.loop(0, dp_count)
+    def _(step):
+        for side in (0, 1):
+            near_copy(side, step).start()
+            own_copy(side, step).start()
+
+    accum[...] = jnp.zeros_like(accum)
+    for side in (0, 1):
+        weight_copy(side, 0).wait_recv()
+        weight_copy(side, 1).start()
+
+    def run(step, first, final, forward):
+        for side in (0, 1):
+            if forward is None:
+                pass
+            elif forward:
+                weight_copy(side, step + 1).wait_recv()
+                weight_copy(side, step + 2).start()
+            else:
+                weight_copy(side, step + 1).wait_recv()
+        for side in (0, 1):
+            for away in range(chip_count - 1):
+                far_copy(away, side, step).wait_recv()
+                pass_copy(away, side, step).start()
+        for side in (0, 1):
+            own_copy(side, step).wait()
+            near_copy(side, step).wait_recv()
+            if final:
+                own_weight(side).wait()
+        for side in (0, 1):
+            for away in range(chip_count - 1):
+                pass_copy(away, side, step).wait_recv()
+            part = jnp.dot(
+                out_t_ref[...], grads[side, step], preferred_element_type=jnp.float32
+            )
+            if not first:
+                sum_copy(side, step - 1).wait_recv()
+                part = part + sums_in[side, step - 1].astype(jnp.float32)
+            if final:
+                weight_grad_ref[:, side * half : (side + 1) * half] = part
+            else:
+                sums_out[side, step] = part.astype(jnp.bfloat16)
+                sum_copy(side, step).start()
+        both = (((1,), (1,)), ((), ()))
+        total = accum[...]
+        for side in (0, 1):
+            total += lax.dot_general(
+                grads[side, step], weights[side, step], both, preferred_element_type=jnp.float32
+            )
+        if final:
+            out_grad_ref[...] = total.astype(jnp.bfloat16)
+        else:
+            accum[...] = total
+
+    run(0, True, False, True)
+
+    @pl.loop(1, dp_count - 3)
+    def _(step):
+        run(step, False, False, True)
+
+    run(dp_count - 3, False, False, False)
+    run(dp_count - 2, False, False, None)
+    run(dp_count - 1, False, True, None)
+
+    @pl.loop(0, dp_count)
+    def _(step):
+        for side in (0, 1):
+            near_copy(side, step).wait_send()
+            for away in range(chip_count - 1):
+                far_copy(away, side, step).wait_send()
+                pass_copy(away, side, step).wait_send()
+
+    @pl.loop(1, dp_count - 1)
+    def _(step):
+        for side in (0, 1):
+            weight_copy(side, step).wait_send()
+            sum_copy(side, step).wait_send()
+
+    for side in (0, 1):
+        weight_copy(side, 0).wait_send()
+        sum_copy(side, 0).wait_send()
+
+
+def exchange(grad_rows, out_weight, out_t):
+    dp_count, tensor_count = lax.axis_size("dp"), lax.axis_size("tensor")
+    far = tensor_count // 2 - 1
+    rows = grad_rows.shape[0]
+    seq_len = rows * tensor_count
+    depth, width = out_weight.shape
+    half = width // 2
+    dma = pltpu.SemaphoreType.DMA
+    vmem = pl.BlockSpec(memory_space=pltpu.VMEM)
+    return pl.pallas_call(
+        functools.partial(exchange_kernel, dp_count, tensor_count),
+        out_shape=(
+            jax.ShapeDtypeStruct((seq_len, depth), jnp.bfloat16),
+            jax.ShapeDtypeStruct((depth, width), jnp.float32),
+        ),
+        in_specs=[pl.BlockSpec(memory_space=pl.ANY), pl.BlockSpec(memory_space=pl.ANY), vmem],
+        out_specs=(vmem, vmem),
+        scratch_shapes=[
+            pltpu.VMEM((2, dp_count, seq_len, half), jnp.bfloat16),
+            pltpu.VMEM((2, dp_count, depth, half), jnp.bfloat16),
+            pltpu.VMEM((2, dp_count - 1, depth, half), jnp.bfloat16),
+            pltpu.VMEM((2, dp_count - 1, depth, half), jnp.bfloat16),
+            pltpu.VMEM((seq_len, depth), jnp.float32),
+            dma((2, dp_count)),
+            dma((2,)),
+            dma((2, dp_count)),
+            dma((2, dp_count)),
+            dma((far, 2, dp_count)),
+            dma((far, 2, dp_count)),
+            dma((far, 2, dp_count)),
+            dma((far, 2, dp_count)),
+            dma((2, dp_count - 1)),
+            dma((2, dp_count - 1)),
+            dma((2, dp_count - 1)),
+            dma((2, dp_count - 1)),
+        ],
+        compiler_params=pltpu.CompilerParams(
+            collective_id=0, has_side_effects=True, vmem_limit_bytes=60 * 1024 * 1024
+        ),
+        name="exchange",
+    )(grad_rows, out_weight, out_t)
 
 
 def swapped(value, axis, apart):
@@ -27,7 +308,6 @@
     doc_ids = jnp.sum((positions[:, None] >= doc_ends[None, :]).astype(jnp.int32), axis=1)
     block_rows = min(512, seq_len)
     block_count = seq_len // block_rows
-    full_weight = lax.all_gather(out_weight, "dp", axis=1, tiled=True)
 
     def key_reach():
         return seq_len
@@ -60,13 +340,7 @@
         totals_list.append(log_total)
     attn_out = jnp.concatenate(outputs_list, axis=1)
     out_flat = attn_out.transpose(1, 0, 2).reshape(seq_len, head_count * HEAD_SIZE)
-    local_rows = grad_out[0]
-    gathered = lax.all_gather(local_rows, "tensor", axis=0, tiled=True)
-    out_grad = jnp.einsum(
-        "sd,hd->sh", gathered, full_weight, preferred_element_type=jnp.float32
-    ).astype(jnp.bfloat16)
-    weight_part = jnp.einsum("sh,sd->hd", out_flat, gathered, preferred_element_type=jnp.float32)
-    weight_grad = lax.psum_scatter(weight_part, "dp", scatter_dimension=1, tiled=True)
+    out_grad, weight_grad = exchange(grad_out[0], out_weight, out_flat.T)
     grad_heads = out_grad.reshape(seq_len, head_count, HEAD_SIZE).transpose(1, 0, 2)
     key_accum = jnp.zeros((seq_len, HEAD_SIZE), jnp.float32)
     value_accum = jnp.zeros((seq_len, HEAD_SIZE), jnp.float32)

time: 375 us -> 138 us (0.37)
  waiting for transfers between devices: 307 us -> 0.01 us
  Pallas kernels: 0 us -> 102 us
  matrix products: 42.1 us -> 19.1 us
  between operations: 14.1 us -> 0.96 us
  local copies, waits for them, and re-layouts: 3.81 us -> 7.76 us
    all_gather x2 -> x0, waiting for transfers between devices: 175 us -> none  [the longest x1 108 us: shards(): gathered = lax.all_gather(local_rows, 'tensor', axis=0, tiled=True)]
    reduce_scatter x1 -> x0, waiting for transfers between devices: 131 us -> none  [shards(): lax.psum_scatter(weight_part, 'dp', scatter_dimension=1, tiled=True)]
    pallas_call x0 -> x1, Pallas kernels: none -> 102 us  [exchange(): pl.pallas_call(functools.partial(exchange_kernel, dp_count, tensor_count)...]
    dot_general x2 -> x0, matrix products: 23.9 us -> none  [the longest x1 12.5 us: shards(): jnp.einsum('sh,sd->hd', out_flat, gathered, preferred_element_type=jnp.fl...]
  transfers between devices with their start and end apart: 5 -> 2, of which waited for: 3 -> 0; matrix products, arithmetic and copies ran while one was open for 6% -> 9% of each run, Pallas kernels for 0% -> 0%
where the time goes in v1:
time: 138 us
  Pallas kernels  102 us (74%)
  matrix products  19.1 us (14%)
  other arithmetic  7.81 us (6%)
  local copies, waits for them, and re-layouts  7.76 us (6%)
    pallas_call x1, Pallas kernels, exchange(): pl.pallas_call(functools.partial(exchange_kernel, dp_count, tensor_count)...  102 us
    dot_general x2, matrix products, shards(): jnp.einsum('hqd,kd->hqk', grad_block, value_rows, preferred_element_type=...  5.73 us
    dot_general x2, matrix products, shards(): jnp.einsum('hqk,hqd->kd', prob_bf16, grad_block, preferred_element_type=j...  5.42 us
    unnamed x19, local copies, waits for them, and re-layouts  3.28 us
    dot_general x2, matrix products, shards(): jnp.einsum('hqk,kd->hqd', prob_bf16, value_rows, preferred_element_type=j...  3.13 us
  transfers between devices with their start and end apart: 2, of which 0 were waited for; matrix products, arithmetic and copies ran while one was open for 9% of the time, Pallas kernels for 0%

profile of v1, /device:TPU:1, one launch (start us, length us, event | category | flops | bytes accessed | tf_op | source)
XLA Modules:
  0.0 137.8 jit_solution(12583883461352381012)
XLA Ops:
  0.6 0.0 copy-start
  0.7 0.9 reduce-window.8
  1.5 0.1 convert_reduce_fusion
  1.7 1.2 copy.30
  2.9 0.3 copy.31
  3.2 0.9 fusion.5
  4.1 0.0 copy-done
  4.1 0.9 fusion.2
  5.1 0.0 copy-start.3
  5.1 0.9 fusion.3
  6.0 0.0 copy-start.1
  6.0 0.0 copy-start.6
  6.0 2.2 %exponential_reduce_fusion = (f32[2,512]{1,0:T(2,128)S(1)}, f32[2,512]{1,0:T(2,128)S(1)}) fusion(f32[1024,2,512]{2,0,1:T(8,128)S(1)} %get-tuple-element.105, f32[2,512]{1,0:T(2,128)S(1)} %get-tuple-element.104, pred[512,1024]{0,1:T(8,128)(4,1)S(1)} %get-tuple-element.98, f32[2,512]{1,0:T(2,128)S(1)} %get-tuple-element.102, ...), kind=kLoop, calls=%fused_computation.5 | loop fusion | flops 8386560 | bytes 9453568 | tf_op jit(solution)/shard_map/reduce_sum | solution.py:333
  8.2 0.0 copy-done.1
  8.3 0.0 copy-done.6
  8.3 1.6 %convolution_convert_fusion.2 = bf16[2,512,128]{2,1,0:T(8,128)(2,1)S(1)} fusion(bf16[1,1024,256]{2,1,0:T(8,128)(2,1)S(1)} %copy-done.6, s32[]{:T(128)S(6)} %select_n.33, f32[1024,2,512]{2,0,1:T(8,128)S(1)} %get-tuple-element.105, f32[2,512]{1,0:T(2,128)S(1)} %log_add_fusion, pred[512,1024]{0,1:T(8,128)(4,1)S(1)} %get-tuple-element.98), kind=kOutput, calls=%fused_computation.24 | convolution fusion | flops 272760832 | bytes 5246980 | tf_op jit(solution)/shard_map/hqk,kd->hqd/dot_general | solution.py:336
  9.8 0.0 copy-done.3
  9.8 1.6 %convolution_convert_fusion.3 = bf16[2,512,128]{2,1,0:T(8,128)(2,1)S(1)} fusion(bf16[1,1024,256]{2,1,0:T(8,128)(2,1)S(1)} %copy-done.6, s32[]{:T(128)S(6)} %select_n.33, f32[1024,2,512]{2,0,1:T(8,128)S(1)} %get-tuple-element.103, f32[2,512]{1,0:T(2,128)S(1)} %log_add_fusion.1, pred[512,1024]{0,1:T(8,128)(4,1)S(1)} %get-tuple-element.99), kind=kOutput, calls=%fused_computation.25 | convolution fusion | flops 272760832 | bytes 5246980 | tf_op jit(solution)/shard_map/hqk,kd->hqd/dot_general | solution.py:336
  11.5 1.0 copy.34
  12.5 101.6 %exchange.1 = (bf16[1024,256]{1,0:T(8,128)(2,1)}, f32[256,1024]{1,0:T(8,128)}) custom-call(bf16[256,8192]{1,0:T(8,128)(2,1)} %bitcast.88, bf16[256,1024]{1,0:T(8,128)(2,1)} %weight_ref.1, bf16[256,1024]{1,0:T(8,128)(2,1)} %bitcast.89), custom_call_target="tpu_custom_call" | custom-call | tf_op jit(solution)/shard_map/exchange/pallas_call | solution.py:256
  114.1 0.0 copy-start.4
  114.1 1.3 bitcast_bitcast_fusion
  115.4 3.3 %convolution_bitcast_fusion = f32[1024,128]{1,0:T(8,128)S(1)} fusion(bf16[2,1024,128]{2,1,0:T(8,128)(2,1)S(1)} %bitcast_bitcast_fusion, f32[1024,2,512]{2,0,1:T(8,128)} %copy-done.1, f32[2,512]{1,0:T(2,128)S(1)} %log_add_fusion, pred[512,1024]{0,1:T(8,128)(4,1)S(1)} %get-tuple-element.98), kind=kOutput, calls=%fused_computation.16 | convolution fusion | flops 272629760 | bytes 5509120 | tf_op jit(solution)/shard_map/hqk,hqd->kd/dot_general | solution.py:375
  118.7 0.0 copy-done.4
  118.8 2.1 %fusion.7 = f32[1024,128]{1,0:T(8,128)} fusion(f32[1024,128]{1,0:T(8,128)S(1)} %convolution_bitcast_fusion, bf16[2,1024,128]{2,1,0:T(8,128)(2,1)S(1)} %bitcast_bitcast_fusion, f32[1024,2,512]{2,0,1:T(8,128)S(1)} %copy-done.4, f32[2,512]{1,0:T(2,128)S(1)} %log_add_fusion.1, pred[512,1024]{0,1:T(8,128)(4,1)S(1)} %get-tuple-element.99), kind=kOutput, calls=%fused_computation.21 | convolution fusion | flops 272760832 | bytes 6033408 | tf_op jit(solution)/shard_map/hqk,hqd->kd/dot_general | solution.py:375
  120.8 1.0 constant_dynamic-slice_fusion
  121.8 0.1 collective-permute-start.1
  121.9 0.4 multiply_reduce_fusion.1
  122.2 0.0 copy-start.2
  122.3 0.0 copy-start.7
  122.3 4.0 %multiply_convert_fusion.1 = bf16[2,512,1024]{1,2,0:T(8,128)(2,1)S(1)} fusion(f32[1024,2,512]{2,0,1:T(8,128)} %copy-done.3, f32[2,512]{1,0:T(2,128)S(1)} %get-tuple-element.96, f32[2,512]{1,0:T(2,128)S(1)} %log_add_fusion.1, pred[512,1024]{0,1:T(8,128)(4,1)S(1)} %get-tuple-element.99, bf16[2,1024,128]{2,1,0:T(8,128)(2,1)S(1)} %bitcast_bitcast_fusion, ...), kind=kOutput, calls=%fused_computation.3 | convolution fusion | flops 275775488 | bytes 7348228 | tf_op jit(solution)/shard_map/hqd,kd->hqk/dot_general | solution.py:357
  126.3 0.0 copy-done.2
  126.3 0.0 copy-done.7
  126.3 1.7 %multiply_convert_fusion = bf16[2,512,1024]{1,2,0:T(8,128)(2,1)S(1)} fusion(f32[1024,2,512]{2,0,1:T(8,128)S(1)} %copy-done.2, f32[2,512]{1,0:T(2,128)S(1)} %get-tuple-element.97, f32[2,512]{1,0:T(2,128)S(1)} %log_add_fusion, pred[512,1024]{0,1:T(8,128)(4,1)S(1)} %get-tuple-element.98, bf16[2,1024,128]{2,1,0:T(8,128)(2,1)S(1)} %bitcast_bitcast_fusion, ...), kind=kOutput, calls=%fused_computation.2 | convolution fusion | flops 275775488 | bytes 7348228 | tf_op jit(solution)/shard_map/hqd,kd->hqk/dot_general | solution.py:357
  128.0 0.7 convolution_bitcast_fusion.2
  128.7 0.7 fusion.6
  129.5 0.7 constant_dynamic-slice_fusion.1
  130.2 0.5 collective-permute-start
  130.7 0.8 convolution_convert_fusion.1
  131.4 0.0 copy-start.5
  131.5 0.8 convolution_convert_fusion
  132.3 0.2 copy.40
  132.5 1.0 copy.41
  133.5 0.0 collective-permute-done.1
  133.5 1.7 %fusion.35 = bf16[1,1,512,128]{3,2,1,0:T(8,128)(2,1)} fusion(f32[512,128]{1,0:T(8,128)} %collective-permute-done.1, f32[1024,128]{1,0:T(8,128)} %fusion.7, s32[]{:T(128)S(6)} %select_n.37), kind=kLoop, calls=%fused_computation.60 | loop fusion | flops 131072 | bytes 655364 | tf_op jit(solution)/shard_map/reshape | solution.py:394
  135.2 0.0 collective-permute-done
  135.2 1.6 %fusion.34 = bf16[1,1,512,128]{3,2,1,0:T(8,128)(2,1)} fusion(f32[512,128]{1,0:T(8,128)} %collective-permute-done, f32[1024,128]{1,0:T(8,128)S(1)} %fusion.6, s32[]{:T(128)S(6)} %select_n.37), kind=kLoop, calls=%fused_computation.59 | loop fusion | flops 131072 | bytes 655364 | tf_op jit(solution)/shard_map/reshape | solution.py:393
  136.8 0.0 copy-done.5
  136.8 1.0 copy.51
  (9 shorter events, 0.1 us)
Async XLA Ops:
  0.6 3.5 %copy-start = (bf16[1,1024,256]{2,1,0:T(8,128)(2,1)S(1)}, bf16[1,1024,256]{2,1,0:T(8,128)(2,1)}, u32[]{:S(2)}) copy-start(bf16[1,1024,256]{2,1,0:T(8,128)(2,1)} %param.23) | copy-start | bytes 1572868
  5.1 4.8 %copy-start.3 = (f32[1024,2,512]{2,0,1:T(8,128)}, f32[1024,2,512]{2,0,1:T(8,128)S(1)}, u32[]{:S(2)}) copy-start(f32[1024,2,512]{2,0,1:T(8,128)S(1)} %get-tuple-element.103) | copy-start | bytes 12582916
  6.0 2.2 %copy-start.1 = (f32[1024,2,512]{2,0,1:T(8,128)}, f32[1024,2,512]{2,0,1:T(8,128)S(1)}, u32[]{:S(2)}) copy-start(f32[1024,2,512]{2,0,1:T(8,128)S(1)} %get-tuple-element.105) | copy-start | bytes 12582916
  6.0 2.2 %copy-start.6 = (bf16[1,1024,256]{2,1,0:T(8,128)(2,1)S(1)}, bf16[1,1024,256]{2,1,0:T(8,128)(2,1)}, u32[]{:S(2)}) copy-start(bf16[1,1024,256]{2,1,0:T(8,128)(2,1)} %param.24) | copy-start | bytes 1572868
  114.1 4.6 %copy-start.4 = (f32[1024,2,512]{2,0,1:T(8,128)S(1)}, f32[1024,2,512]{2,0,1:T(8,128)}, u32[]{:S(2)}) copy-start(f32[1024,2,512]{2,0,1:T(8,128)} %copy-done.3) | copy-start | bytes 12582916
  121.8 11.7 %collective-permute-start.1 = (f32[512,128]{1,0:T(8,128)S(1)}, f32[512,128]{1,0:T(8,128)}, u32[]{:S(2)}, u32[]{:S(2)}) collective-permute-start(f32[512,128]{1,0:T(8,128)S(1)} %constant_dynamic-slice_fusion), channel_id=1, source_target_pairs={{0,1},{1,0},{2,3},{3,2},{4,5},{5,4},{6,7},{7,6},{8,9},{9,8},{10,11... | collective-permute-start | bytes 786440 | tf_op jit(solution)/shard_map/ppermute | solution.py:293
  122.2 4.1 %copy-start.2 = (f32[1024,2,512]{2,0,1:T(8,128)S(1)}, f32[1024,2,512]{2,0,1:T(8,128)}, u32[]{:S(2)}) copy-start(f32[1024,2,512]{2,0,1:T(8,128)} %copy-done.1) | copy-start | bytes 12582916
  122.3 4.1 %copy-start.7 = (bf16[1,1024,256]{2,1,0:T(8,128)(2,1)S(1)}, bf16[1,1024,256]{2,1,0:T(8,128)(2,1)}, u32[]{:S(2)}) copy-start(bf16[1,1024,256]{2,1,0:T(8,128)(2,1)} %param.24) | copy-start | bytes 1572868
  130.2 5.0 %collective-permute-start = (f32[512,128]{1,0:T(8,128)}, f32[512,128]{1,0:T(8,128)}, u32[]{:S(2)}, u32[]{:S(2)}) collective-permute-start(f32[512,128]{1,0:T(8,128)} %constant_dynamic-slice_fusion.1), channel_id=1, source_target_pairs={{0,1},{1,0},{2,3},{3,2},{4,5},{5,4},{6,7},{7,6},{8,9},{9,8},{10,11... | collective-permute-start | bytes 786440 | tf_op jit(solution)/shard_map/ppermute | solution.py:293
  131.4 5.4 %copy-start.5 = (f32[256,1024]{1,0:T(8,128)S(1)}, f32[256,1024]{1,0:T(8,128)}, u32[]{:S(2)}) copy-start(f32[256,1024]{1,0:T(8,128)} %get-tuple-element.115) | copy-start | bytes 3145732

commit v2 on v1

v2 whole, which is shorter than its diff:
```python
import functools

import jax
import jax.numpy as jnp
from jax import lax
from jax.experimental import pallas as pl
from jax.experimental.pallas import tpu as pltpu
from jax.sharding import PartitionSpec as P

HEAD_SIZE = 128


MESH = pl.DeviceIdType.MESH


def ring_place(index, count):
    odd = index % 2
    return (1 - odd) * (index // 2) + odd * (count - 1 - index // 2)


def ring_index(place, count):
    back = place // (count // 2)
    return (1 - back) * (2 * place) + back * (2 * (count - 1 - place) + 1)


def exchange_kernel(
    dp_count,
    tensor_count,
    grad_ref,
    weight_ref,
    query_ref,
    key_ref,
    value_ref,
    lengths_ref,
    query_grad_ref,
    key_grad_ref,
    value_grad_ref,
    weight_grad_ref,
    grads,
    weights,
    sums_out,
    sums_in,
    accum,
    probs,
    outs,
    outs_t,
    kv_grads,
    kv_in,
    own_sem,
    own_weight_sem,
    near_send,
    near_recv,
    far_send,
    far_recv,
    pass_send,
    pass_recv,
    weight_send,
    weight_recv,
    sum_send,
    sum_recv,
    kv_send,
    kv_recv,
):
    dp_index = lax.axis_index("dp")
    tensor_index = lax.axis_index("tensor")
    chip_count = tensor_count // 2
    chip, core = tensor_index // 2, tensor_index % 2
    partner = chip * 2 + 1 - core
    place = ring_place(dp_index, dp_count)
    ring = (
        ring_index((place + 1) % dp_count, dp_count),
        ring_index((place + dp_count - 1) % dp_count, dp_count),
    )
    rows = grad_ref.shape[0]
    half = weight_ref.shape[1] // 2
    last = dp_count - 1
    seq_len, depth = query_ref.shape
    heads = depth // HEAD_SIZE
    half_rows = seq_len // 2
    score_scale = HEAD_SIZE ** (-0.5)
    lead = min(2, dp_count - 2)
    kv_columns = pl.ds(pl.multiple_of(tensor_index // 2 * HEAD_SIZE, HEAD_SIZE), HEAD_SIZE)
    far_chips = [(chip + away) % chip_count for away in range(1, chip_count)]

    def place_rows(index):
        return pl.ds(pl.multiple_of(index * rows, rows), rows)

    def columns(side, step):
        if side == 0:
            owner = ring_index((place + 2 * dp_count - 1 - step) % dp_count, dp_count)
        else:
            owner = ring_index((place + 1 + step) % dp_count, dp_count)
        return pl.ds(pl.multiple_of(owner * (2 * half) + side * half, half), half)

    def own_copy(side, step):
        return pltpu.make_async_copy(
            grad_ref.at[:, columns(side, step)],
            grads.at[side, step, place_rows(tensor_index)],
            own_sem.at[side, step],
        )

    def own_weight(side):
        return pltpu.make_async_copy(
            weight_ref.at[:, pl.ds(side * half, half)],
            weights.at[side, last],
            own_weight_sem.at[side],
        )

    def near_copy(side, step):
        return pltpu.make_async_remote_copy(
            grad_ref.at[:, columns(side, step)],
            grads.at[side, step, place_rows(tensor_index)],
            near_send.at[side, step],
            near_recv.at[side, step],
            device_id=(dp_index, partner),
            device_id_type=MESH,
        )

    def far_copy(away, side, step):
        return pltpu.make_async_remote_copy(
            grad_ref.at[:, columns(side, step)],
            grads.at[side, step, place_rows(tensor_index)],
            far_send.at[away, side, step],
            far_recv.at[away, side, step],
            device_id=(dp_index, far_chips[away] * 2 + core),
            device_id_type=MESH,
        )

    def pass_copy(away, side, step):
        source = (chip + chip_count - 1 - away) % chip_count * 2 + core
        block = grads.at[side, step, place_rows(source)]
        return pltpu.make_async_remote_copy(
            block,
            block,
            pass_send.at[away, side, step],
            pass_recv.at[away, side, step],
            device_id=(dp_index, partner),
            device_id_type=MESH,
        )

    def weight_copy(side, hop):
        if isinstance(hop, int) and hop == 0:
            source = weight_ref.at[:, pl.ds(side * half, half)]
        else:
            source = weights.at[side, hop - 1]
        return pltpu.make_async_remote_copy(
            source,
            weights.at[side, hop],
            weight_send.at[side, hop],
            weight_recv.at[side, hop],
            device_id=(ring[side], tensor_index),
            device_id_type=MESH,
        )

    def sum_copy(side, step):
        return pltpu.make_async_remote_copy(
            sums_out.at[side, step],
            sums_in.at[side, step],
            sum_send.at[side, step],
            sum_recv.at[side, step],
            device_id=(ring[side], tensor_index),
            device_id_type=MESH,
        )

    targets = [(dp_index, partner), (ring[0], tensor_index), (ring[1], tensor_index)]
    targets += [(dp_index, other * 2 + core) for other in far_chips]
    barrier = pltpu.get_barrier_semaphore()
    for target in targets:
        pl.semaphore_signal(barrier, inc=1, device_id=target, device_id_type=MESH)
    pl.semaphore_wait(barrier, len(targets))

    for side in (0, 1):
        weight_copy(side, 0).start()
        own_weight(side).start()

    @pl.loop(0, dp_count)
    def _(step):
        for side in (0, 1):
            for away in range(chip_count - 1):
                far_copy(away, side, step).start()

    @pl.loop(0, dp_count)
    def _(step):
        for side in (0, 1):
            near_copy(side, step).start()
            own_copy(side, step).start()

    kv_copy = pltpu.make_async_remote_copy(
        kv_grads.at[:, pl.ds(pl.multiple_of((1 - core) * half_rows, half_rows), half_rows)],
        kv_in,
        kv_send,
        kv_recv,
        device_id=(dp_index, partner),
        device_id_type=MESH,
    )
    accum[...] = jnp.zeros_like(accum)
    kv_grads[...] = jnp.zeros_like(kv_grads)
    nt = (((1,), (1,)), ((), ()))
    tn = (((0,), (0,)), ((), ()))

    def dot(left, right, dims):
        return lax.dot_general(left, right, dims, preferred_element_type=jnp.float32)

    def forward(block, size):
        here = pl.ds(pl.multiple_of(block * size, size), size)
        query_places = block * size + lax.broadcasted_iota(jnp.int32, (size, 1), 0)
        key_places = lax.broadcasted_iota(jnp.int32, (size, seq_len), 1)
        doc_start = jnp.zeros((size, 1), jnp.int32)
        doc_end = jnp.int32(0)
        for doc in range(lengths_ref.shape[1]):
            doc_end = doc_end + lengths_ref[0, doc]
            doc_start = jnp.where(query_places >= doc_end, doc_end, doc_start)
        allowed = (key_places >= doc_start) & (key_places <= query_places)
        keys, values = key_ref[:, kv_columns], value_ref[:, kv_columns]
        for head in range(heads):
            lanes = slice(head * HEAD_SIZE, (head + 1) * HEAD_SIZE)
            scores = dot(query_ref[here, lanes], keys, nt) * score_scale
            scores = jnp.where(allowed, scores, -jnp.inf)
            row_max = jnp.max(scores, axis=1, keepdims=True)
            total = jnp.sum(jnp.exp(scores - row_max), axis=1, keepdims=True)
            prob = jnp.exp(scores - (row_max + jnp.log(total)))
            probs[head, here] = prob
            out = jnp.dot(prob.astype(jnp.bfloat16), values, preferred_element_type=jnp.float32)
            outs[here, lanes] = out.astype(jnp.bfloat16)
            outs_t[lanes, here] = out.T.astype(jnp.bfloat16)

    def backward(block):
        here = place_rows(block)
        keys, values = key_ref[:, kv_columns], value_ref[:, kv_columns]
        for head in range(heads):
            lanes = slice(head * HEAD_SIZE, (head + 1) * HEAD_SIZE)
            grad = accum[here, lanes].astype(jnp.bfloat16)
            delta = jnp.sum(
                grad.astype(jnp.float32) * outs[here, lanes].astype(jnp.float32), axis=1, keepdims=True
            )
            prob = probs[head, here]
            dscore = (prob * (dot(grad, values, nt) - delta) * score_scale).astype(jnp.bfloat16)
            query_grad_ref[here, lanes] = jnp.dot(
                dscore, keys, preferred_element_type=jnp.float32
            ).astype(jnp.bfloat16)
            kv_grads[0] += dot(dscore, query_ref[here, lanes], tn)
            kv_grads[1] += dot(prob.astype(jnp.bfloat16), grad, tn)

    def project(owner_chip, step):
        here = pl.ds(pl.multiple_of(owner_chip * (2 * rows), 2 * rows), 2 * rows)
        total = accum[here]
        for side in (0, 1):
            total += dot(grads[side, step, here], weights[side, step], nt)
        accum[here] = total

    def local_step(step):
        for side in (0, 1):
            own_copy(side, step).wait()
            near_copy(side, step).wait_recv()
        project(chip, step)

    def weight_step(hop, send):
        for side in (0, 1):
            weight_copy(side, hop).wait_recv()
            if send:
                weight_copy(side, hop + 1).start()

    def far_step(step):
        for side in (0, 1):
            for away in range(chip_count - 1):
                far_copy(away, side, step).wait_recv()
                pass_copy(away, side, step).start()
        for side in (0, 1):
            for away in range(chip_count - 1):
                pass_copy(away, side, step).wait_recv()

    def sum_step(step, first, final):
        for side in (0, 1):
            part = jnp.dot(
                outs_t[...], grads[side, step], preferred_element_type=jnp.float32
            )
            if not first:
                sum_copy(side, step - 1).wait_recv()
                part = part + sums_in[side, step - 1].astype(jnp.float32)
            if final:
                weight_grad_ref[:, side * half : (side + 1) * half] = part
            else:
                sums_out[side, step] = part.astype(jnp.bfloat16)
                sum_copy(side, step).start()

    def far_project(step):
        for other in far_chips:
            project(other, step)

    block_rows = min(256, seq_len)
    blocks = seq_len // block_rows

    @pl.loop(0, blocks // 2)
    def _(block):
        forward(block, block_rows)

    weight_step(0, dp_count > 2)

    @pl.loop(blocks // 2, blocks)
    def _(block):
        forward(block, block_rows)

    for hop in range(1, lead):
        weight_step(hop, hop < last - 1)
    for side in (0, 1):
        own_weight(side).wait()
    local_step(last)
    for step in range(lead):
        local_step(step)

    def step_with_weights(step, first, send):
        weight_step(step + lead, send)
        local_step(step + lead)
        far_step(step)
        sum_step(step, first, False)
        far_project(step)

    step_with_weights(0, True, lead < last - 1)

    @pl.loop(1, last - 1 - lead)
    def _(step):
        step_with_weights(step, False, True)

    if last - 1 - lead > 0:
        step_with_weights(last - 1 - lead, False, False)

    for step in range(last - lead, last):
        far_step(step)
        sum_step(step, False, False)
        far_project(step)
        if step == last - lead:

            @pl.loop(0, 2)
            def _(block):
                backward(chip * 2 + block)

    far_step(last)
    far_project(last)

    @pl.loop(0, tensor_count - 2)
    def _(block):
        backward((chip * 2 + 2 + block) % tensor_count)

    kv_copy.start()
    sum_step(last, False, True)
    kv_copy.wait()
    mine = pl.ds(pl.multiple_of(core * half_rows, half_rows), half_rows)
    key_grad_ref[...] = (kv_grads[0, mine] + kv_in[0]).astype(jnp.bfloat16)
    value_grad_ref[...] = (kv_grads[1, mine] + kv_in[1]).astype(jnp.bfloat16)

    @pl.loop(0, dp_count)
    def _(step):
        for side in (0, 1):
            near_copy(side, step).wait_send()
            for away in range(chip_count - 1):
                far_copy(away, side, step).wait_send()
                pass_copy(away, side, step).wait_send()

    @pl.loop(1, dp_count - 1)
    def _(step):
        for side in (0, 1):
            weight_copy(side, step).wait_send()
            sum_copy(side, step).wait_send()

    for side in (0, 1):
        weight_copy(side, 0).wait_send()
        sum_copy(side, 0).wait_send()


def shards(query_act, rotated_keys, value_input, grad_out, out_weight, doc_lengths):
    dp_count, tensor_count = lax.axis_size("dp"), lax.axis_size("tensor")
    far = tensor_count // 2 - 1
    seq_len = query_act.shape[1]
    depth, width = out_weight.shape
    half = width // 2
    dma = pltpu.SemaphoreType.DMA
    vmem = pl.BlockSpec(memory_space=pltpu.VMEM)
    anywhere = pl.BlockSpec(memory_space=pl.ANY)
    kv_shape = jax.ShapeDtypeStruct((seq_len // 2, HEAD_SIZE), jnp.bfloat16)
    query_grad, key_grad, value_grad, weight_grad = pl.pallas_call(
        functools.partial(exchange_kernel, dp_count, tensor_count),
        out_shape=(
            jax.ShapeDtypeStruct((seq_len, depth), jnp.bfloat16),
            kv_shape,
            kv_shape,
            jax.ShapeDtypeStruct((depth, width), jnp.float32),
        ),
        in_specs=[
            anywhere,
            anywhere,
            vmem,
            vmem,
            vmem,
            pl.BlockSpec(memory_space=pltpu.SMEM),
        ],
        out_specs=(vmem, vmem, vmem, vmem),
        scratch_shapes=[
            pltpu.VMEM((2, dp_count, seq_len, half), jnp.bfloat16),
            pltpu.VMEM((2, dp_count, depth, half), jnp.bfloat16),
            pltpu.VMEM((2, dp_count - 1, depth, half), jnp.bfloat16),
            pltpu.VMEM((2, dp_count - 1, depth, half), jnp.bfloat16),
            pltpu.VMEM((seq_len, depth), jnp.float32),
            pltpu.VMEM((depth // HEAD_SIZE, seq_len, seq_len), jnp.float32),
            pltpu.VMEM((seq_len, depth), jnp.bfloat16),
            pltpu.VMEM((depth, seq_len), jnp.bfloat16),
            pltpu.VMEM((2, seq_len, HEAD_SIZE), jnp.float32),
            pltpu.VMEM((2, seq_len // 2, HEAD_SIZE), jnp.float32),
            dma((2, dp_count)),
            dma((2,)),
            dma((2, dp_count)),
            dma((2, dp_count)),
            dma((far, 2, dp_count)),
            dma((far, 2, dp_count)),
            dma((far, 2, dp_count)),
            dma((far, 2, dp_count)),
            dma((2, dp_count - 1)),
            dma((2, dp_count - 1)),
            dma((2, dp_count - 1)),
            dma((2, dp_count - 1)),
            dma,
            dma,
        ],
        compiler_params=pltpu.CompilerParams(
            collective_id=0, has_side_effects=True, vmem_limit_bytes=60 * 1024 * 1024
        ),
        name="exchange",
    )(grad_out[0], out_weight, query_act[0], rotated_keys[0], value_input[0], doc_lengths)
    return (query_grad[None], key_grad[None, None], value_grad[None, None], weight_grad)


def solution(mesh):
    placed = (
        P("dp", None, "tensor"),
        P("dp", None, None),
        P("dp", None, None),
        P("dp", "tensor", None),
        P("tensor", "dp"),
        P("dp", None),
    )
    return jax.shard_map(
        shards,
        mesh=mesh,
        in_specs=placed,
        out_specs=(
            P("dp", None, "tensor"),
            P("dp", "tensor", None, None),
            P("dp", "tensor", None, None),
            P("tensor", "dp"),
        ),
        check_vma=False,
    )
```

time: 138 us -> 114 us (0.83)
  matrix products: 19.1 us -> 0 us
  other arithmetic: 7.81 us -> 0 us
  Pallas kernels: 102 us -> 105 us
    dot_general x12 -> x0, matrix products: 19.1 us -> none  [the longest x2 5.73 us: shards(): jnp.einsum('hqd,kd->hqk', grad_block, value_rows, preferred_element_type=...]
    unnamed x19 -> x4, local copies, waits for them, and re-layouts: 3.28 us -> 7.31 us
    pallas_call x1, Pallas kernels: 102 us -> 105 us  [shards(): pl.pallas_call(functools.partial(exchange_kernel, dp_count, tensor_count)...]
    reshape x2 -> x0, other arithmetic: 3.35 us -> none  [the longest x1 1.71 us: shards(): value_mine.astype(jnp.bfloat16).reshape(1, 1, half_rows, HEAD_SIZE)]
    reduce_sum x3 -> x0, other arithmetic: 2.6 us -> none  [the longest x1 2.16 us: shards(): jnp.sum(jnp.exp(scores - row_max), axis=-1, keepdims=True)]
    transpose x3 -> x0, local copies, waits for them, and re-layouts: 2.51 us -> none  [the longest x1 1.28 us: shards(): out_grad.reshape(seq_len, head_count, HEAD_SIZE).transpose(1, 0, 2)]
    dynamic_slice x2 -> x0, local copies, waits for them, and re-layouts: 1.68 us -> none  [the longest x1 0.97 us: shards(): lax.dynamic_slice_in_dim(value_accum, other_start, half_rows, 0)]
  transfers between devices with their start and end apart: 2 -> 0, of which waited for: 0 -> 0; matrix products, arithmetic and copies ran while one was open for 9% -> 0% of each run, Pallas kernels for 0% -> 0%
where the time goes in v2:
time: 114 us; the launch traced here: 113 us
  Pallas kernels  105 us (92%)
  local copies, waits for them, and re-layouts  7.31 us (6%)
    pallas_call x1, Pallas kernels, shards(): pl.pallas_call(functools.partial(exchange_kernel, dp_count, tensor_count)...  105 us
    unnamed x4, local copies, waits for them, and re-layouts  7.31 us

profile of v2, /device:TPU:1, one launch (start us, length us, event | category | flops | bytes accessed | tf_op | source)
XLA Modules:
  0.0 113.3 jit_solution(15020227871584039124)
XLA Ops:
  0.6 105.3 %exchange.1 = (bf16[1024,256]{1,0:T(8,128)(2,1)}, bf16[512,128]{1,0:T(8,128)(2,1)}, bf16[512,128]{1,0:T(8,128)(2,1)}, f32[256,1024]{1,0:T(8,128)}) custom-call(bf16[256,8192]{1,0:T(8,128)(2,1)} %bitcast.7, bf16[256,1024]{1,0:T(8,128)(2,1)} %weight_ref.1, bf16[1024,256]{1,0:T(8,128)(2,1)} %bitcast.8, bf16[1024,256]{1,0:T(8,128)(2,1)} %bitcast.9, ...), custom_call_target="tpu_custom_call" | custom-call | tf_op jit(solution)/shard_map/exchange/pallas_call | solution.py:380
  106.0 1.9 %copy.14 = bf16[1,1024,256]{2,1,0:T(8,128)(2,1)} copy(bf16[1,1024,256]{2,1,0:T(8,128)(2,1)} %bitcast.11) | data formatting | bytes 1048576
  107.8 1.6 %copy.15 = bf16[1,1,512,128]{3,2,1,0:T(8,128)(2,1)} copy(bf16[1,1,512,128]{3,2,1,0:T(8,128)(2,1)} %bitcast.13) | data formatting | bytes 262144
  109.4 1.6 %copy.16 = bf16[1,1,512,128]{3,2,1,0:T(8,128)(2,1)} copy(bf16[1,1,512,128]{3,2,1,0:T(8,128)(2,1)} %bitcast.12) | data formatting | bytes 262144
  111.0 2.3 %copy.17 = f32[256,1024]{1,0:T(8,128)} copy(f32[256,1024]{1,0:T(8,128)} %get-tuple-element.19) | data formatting | bytes 2097152

commit v3 on v2

--- a/solution.py
+++ b/solution.py
@@ -28,9 +28,9 @@
     tensor_count,
     grad_ref,
     weight_ref,
-    query_ref,
-    key_ref,
-    value_ref,
+    query_full,
+    key_full,
+    value_full,
     lengths_ref,
     query_grad_ref,
     key_grad_ref,
@@ -41,7 +41,11 @@
     sums_out,
     sums_in,
     accum,
+    query_ref,
+    key_ref,
+    value_ref,
     probs,
+    dscores,
     outs,
     outs_t,
     kv_grads,
@@ -60,6 +64,7 @@
     sum_recv,
     kv_send,
     kv_recv,
+    load_sem,
 ):
     dp_index = lax.axis_index("dp")
     tensor_index = lax.axis_index("tensor")
@@ -74,7 +79,7 @@
     rows = grad_ref.shape[0]
     half = weight_ref.shape[1] // 2
     last = dp_count - 1
-    seq_len, depth = query_ref.shape
+    seq_len, depth = query_full.shape
     heads = depth // HEAD_SIZE
     half_rows = seq_len // 2
     score_scale = HEAD_SIZE ** (-0.5)
@@ -162,6 +167,14 @@
             device_id_type=MESH,
         )
 
+    loads = [
+        pltpu.make_async_copy(query_full, query_ref, load_sem.at[0]),
+        pltpu.make_async_copy(key_full.at[:, kv_columns], key_ref, load_sem.at[1]),
+        pltpu.make_async_copy(value_full.at[:, kv_columns], value_ref, load_sem.at[2]),
+    ]
+    for load in loads:
+        load.start()
+
     targets = [(dp_index, partner), (ring[0], tensor_index), (ring[1], tensor_index)]
     targets += [(dp_index, other * 2 + core) for other in far_chips]
     barrier = pltpu.get_barrier_semaphore()
@@ -169,15 +182,19 @@
         pl.semaphore_signal(barrier, inc=1, device_id=target, device_id_type=MESH)
     pl.semaphore_wait(barrier, len(targets))
 
+    def far_start(step):
+        for side in (0, 1):
+            for away in range(chip_count - 1):
+                far_copy(away, side, step).start()
+
+    far_start(0)
     for side in (0, 1):
         weight_copy(side, 0).start()
         own_weight(side).start()
 
-    @pl.loop(0, dp_count)
+    @pl.loop(1, dp_count)
     def _(step):
-        for side in (0, 1):
-            for away in range(chip_count - 1):
-                far_copy(away, side, step).start()
+        far_start(step)
 
     @pl.loop(0, dp_count)
     def _(step):
@@ -211,7 +228,7 @@
             doc_end = doc_end + lengths_ref[0, doc]
             doc_start = jnp.where(query_places >= doc_end, doc_end, doc_start)
         allowed = (key_places >= doc_start) & (key_places <= query_places)
-        keys, values = key_ref[:, kv_columns], value_ref[:, kv_columns]
+        keys, values = key_ref[...], value_ref[...]
         for head in range(heads):
             lanes = slice(head * HEAD_SIZE, (head + 1) * HEAD_SIZE)
             scores = dot(query_ref[here, lanes], keys, nt) * score_scale
@@ -224,9 +241,8 @@
             outs[here, lanes] = out.astype(jnp.bfloat16)
             outs_t[lanes, here] = out.T.astype(jnp.bfloat16)
 
-    def backward(block):
+    def score_grads(block):
         here = place_rows(block)
-        keys, values = key_ref[:, kv_columns], value_ref[:, kv_columns]
         for head in range(heads):
             lanes = slice(head * HEAD_SIZE, (head + 1) * HEAD_SIZE)
             grad = accum[here, lanes].astype(jnp.bfloat16)
@@ -234,15 +250,37 @@
                 grad.astype(jnp.float32) * outs[here, lanes].astype(jnp.float32), axis=1, keepdims=True
             )
             prob = probs[head, here]
-            dscore = (prob * (dot(grad, values, nt) - delta) * score_scale).astype(jnp.bfloat16)
+            dscore = prob * (dot(grad, value_ref[...], nt) - delta) * score_scale
+            dscores[head, here] = dscore.astype(jnp.bfloat16)
+
+    def chip_rows(owner_chip):
+        return pl.ds(pl.multiple_of(owner_chip * (2 * rows), 2 * rows), 2 * rows)
+
+    def kv_part(owner_chip, part):
+        here = chip_rows(owner_chip)
+        to = pl.ds(pl.multiple_of(part * half_rows, half_rows), half_rows)
+        key_total, value_total = kv_grads[0, to], kv_grads[1, to]
+        for head in range(heads):
+            lanes = slice(head * HEAD_SIZE, (head + 1) * HEAD_SIZE)
+            key_total += dot(dscores[head, here, to], query_ref[here, lanes], tn)
+            value_total += dot(
+                probs[head, here, to].astype(jnp.bfloat16),
+                accum[here, lanes].astype(jnp.bfloat16),
+                tn,
+            )
+        kv_grads[0, to] = key_total
+        kv_grads[1, to] = value_total
+
+    def query_part(owner_chip):
+        here = chip_rows(owner_chip)
+        for head in range(heads):
+            lanes = slice(head * HEAD_SIZE, (head + 1) * HEAD_SIZE)
             query_grad_ref[here, lanes] = jnp.dot(
-                dscore, keys, preferred_element_type=jnp.float32
+                dscores[head, here], key_ref[...], preferred_element_type=jnp.float32
             ).astype(jnp.bfloat16)
-            kv_grads[0] += dot(dscore, query_ref[here, lanes], tn)
-            kv_grads[1] += dot(prob.astype(jnp.bfloat16), grad, tn)
 
     def project(owner_chip, step):
-        here = pl.ds(pl.multiple_of(owner_chip * (2 * rows), 2 * rows), 2 * rows)
+        here = chip_rows(owner_chip)
         total = accum[here]
         for side in (0, 1):
             total += dot(grads[side, step, here], weights[side, step], nt)
@@ -287,6 +325,8 @@
         for other in far_chips:
             project(other, step)
 
+    for load in loads:
+        load.wait()
     block_rows = min(256, seq_len)
     blocks = seq_len // block_rows
 
@@ -332,16 +372,25 @@
 
             @pl.loop(0, 2)
             def _(block):
-                backward(chip * 2 + block)
+                score_grads(chip * 2 + block)
+
+            kv_part(chip, 0)
+            kv_part(chip, 1)
+            query_part(chip)
 
     far_step(last)
     far_project(last)
 
     @pl.loop(0, tensor_count - 2)
     def _(block):
-        backward((chip * 2 + 2 + block) % tensor_count)
-
+        score_grads((chip * 2 + 2 + block) % tensor_count)
+
+    for other in far_chips:
+        kv_part(other, 1 - core)
     kv_copy.start()
+    for other in far_chips:
+        kv_part(other, core)
+        query_part(other)
     sum_step(last, False, True)
     kv_copy.wait()
     mine = pl.ds(pl.multiple_of(core * half_rows, half_rows), half_rows)
@@ -365,6 +414,36 @@
     for side in (0, 1):
         weight_copy(side, 0).wait_send()
         sum_copy(side, 0).wait_send()
+
+
+def finish_kernel(*refs):
+    count = (len(refs) - 2) // 3
+    sources, results, held = refs[:count], refs[count : 2 * count], refs[2 * count : 3 * count]
+    in_sem, out_sem = refs[3 * count :]
+    takes = [pltpu.make_async_copy(sources[i], held[i], in_sem.at[i]) for i in range(count)]
+    puts = [pltpu.make_async_copy(held[i], results[i], out_sem.at[i]) for i in range(count)]
+    for take in takes:
+        take.start()
+    for take, put in zip(takes, puts):
+        take.wait()
+        put.start()
+    for put in puts:
+        put.wait()
+
+
+def finish(*values):
+    anywhere = pl.BlockSpec(memory_space=pl.ANY)
+    dma = pltpu.SemaphoreType.DMA
+    return pl.pallas_call(
+        finish_kernel,
+        out_shape=tuple(jax.ShapeDtypeStruct(value.shape, value.dtype) for value in values),
+        in_specs=[anywhere] * len(values),
+        out_specs=(anywhere,) * len(values),
+        scratch_shapes=[pltpu.VMEM(value.shape, value.dtype) for value in values]
+        + [dma((len(values),)), dma((len(values),))],
+        compiler_params=pltpu.CompilerParams(vmem_limit_bytes=62 * 1024 * 1024),
+        name="finish",
+    )(*values)
 
 
 def shards(query_act, rotated_keys, value_input, grad_out, out_weight, doc_lengths):
@@ -388,9 +467,9 @@
         in_specs=[
             anywhere,
             anywhere,
-            vmem,
-            vmem,
-            vmem,
+            anywhere,
+            anywhere,
+            anywhere,
             pl.BlockSpec(memory_space=pltpu.SMEM),
         ],
         out_specs=(vmem, vmem, vmem, vmem),
@@ -400,7 +479,11 @@
             pltpu.VMEM((2, dp_count - 1, depth, half), jnp.bfloat16),
             pltpu.VMEM((2, dp_count - 1, depth, half), jnp.bfloat16),
             pltpu.VMEM((seq_len, depth), jnp.float32),
+            pltpu.VMEM((seq_len, depth), jnp.bfloat16),
+            pltpu.VMEM((seq_len, HEAD_SIZE), jnp.bfloat16),
+            pltpu.VMEM((seq_len, HEAD_SIZE), jnp.bfloat16),
             pltpu.VMEM((depth // HEAD_SIZE, seq_len, seq_len), jnp.float32),
+            pltpu.VMEM((depth // HEAD_SIZE, seq_len, seq_len), jnp.bfloat16),
             pltpu.VMEM((seq_len, depth), jnp.bfloat16),
             pltpu.VMEM((depth, seq_len), jnp.bfloat16),
             pltpu.VMEM((2, seq_len, HEAD_SIZE), jnp.float32),
@@ -419,12 +502,16 @@
             dma((2, dp_count - 1)),
             dma,
             dma,
+            dma((3,)),
         ],
         compiler_params=pltpu.CompilerParams(
             collective_id=0, has_side_effects=True, vmem_limit_bytes=60 * 1024 * 1024
         ),
         name="exchange",
     )(grad_out[0], out_weight, query_act[0], rotated_keys[0], value_input[0], doc_lengths)
+    query_grad, key_grad, value_grad, weight_grad = finish(
+        query_grad, key_grad, value_grad, weight_grad
+    )
     return (query_grad[None], key_grad[None, None], value_grad[None, None], weight_grad)
 
 

time: 114 us -> 108 us (0.947)
  local copies, waits for them, and re-layouts: 7.31 us -> 0 us
  Pallas kernels: 105 us -> 107 us
    unnamed x4 -> x0, local copies, waits for them, and re-layouts: 7.31 us -> none
    pallas_call x0 -> x1, Pallas kernels: none -> 2.51 us  [finish(): pl.pallas_call(finish_kernel, out_shape=tuple((jax.ShapeDtypeStruct(value...]
where the time goes in v3:
time: 108 us
  Pallas kernels  107 us (99%)
    pallas_call x1, Pallas kernels, shards(): pl.pallas_call(functools.partial(exchange_kernel, dp_count, tensor_count)...  105 us
    pallas_call x1, Pallas kernels, finish(): pl.pallas_call(finish_kernel, out_shape=tuple((jax.ShapeDtypeStruct(value...  2.51 us

profile of v3, /device:TPU:1, one launch (start us, length us, event | category | flops | bytes accessed | tf_op | source)
XLA Modules:
  0.0 107.8 jit_solution(5865889987867997530)
XLA Ops:
  0.6 104.5 %exchange.1 = (bf16[1024,256]{1,0:T(8,128)(2,1)}, bf16[512,128]{1,0:T(8,128)(2,1)}, bf16[512,128]{1,0:T(8,128)(2,1)}, f32[256,1024]{1,0:T(8,128)}) custom-call(bf16[256,8192]{1,0:T(8,128)(2,1)} %bitcast.7, bf16[256,1024]{1,0:T(8,128)(2,1)} %weight_ref.1, bf16[1024,256]{1,0:T(8,128)(2,1)} %bitcast.8, bf16[1024,256]{1,0:T(8,128)(2,1)} %bitcast.9, ...), custom_call_target="tpu_custom_call" | custom-call | tf_op jit(solution)/shard_map/exchange/pallas_call | solution.py:459
  105.2 2.5 %finish.1 = (bf16[1024,256]{1,0:T(8,128)(2,1)}, bf16[512,128]{1,0:T(8,128)(2,1)}, bf16[512,128]{1,0:T(8,128)(2,1)}, f32[256,1024]{1,0:T(8,128)}) custom-call(bf16[1024,256]{1,0:T(8,128)(2,1)} %get-tuple-element.12.refs_0_, bf16[512,128]{1,0:T(8,128)(2,1)} %get-tuple-element.13.refs_1_, bf16[512,128]{1,0:T(8,128)(2,1)} %get-tuple-element.14.refs_2_, ...), custom_call_target="tpu_custom_call" | custom-call | tf_op jit(solution)/shard_map/finish/pallas_call | solution.py:437

commit v4 on v3

--- a/solution.py
+++ b/solution.py
@@ -32,10 +32,10 @@
     key_full,
     value_full,
     lengths_ref,
-    query_grad_ref,
+    query_grad_out,
     key_grad_ref,
     value_grad_ref,
-    weight_grad_ref,
+    weight_grad_out,
     grads,
     weights,
     sums_out,
@@ -44,7 +44,10 @@
     query_ref,
     key_ref,
     value_ref,
+    query_grad_ref,
+    weight_grad_ref,
     probs,
+    probs_t,
     dscores,
     outs,
     outs_t,
@@ -65,6 +68,7 @@
     kv_send,
     kv_recv,
     load_sem,
+    out_sem,
 ):
     dp_index = lax.axis_index("dp")
     tensor_index = lax.axis_index("tensor")
@@ -214,6 +218,8 @@
     kv_grads[...] = jnp.zeros_like(kv_grads)
     nt = (((1,), (1,)), ((), ()))
     tn = (((0,), (0,)), ((), ()))
+    nn = (((1,), (0,)), ((), ()))
+    weight_put = pltpu.make_async_copy(weight_grad_ref, weight_grad_out, out_sem.at[chip_count])
 
     def dot(left, right, dims):
         return lax.dot_general(left, right, dims, preferred_element_type=jnp.float32)
@@ -264,12 +270,22 @@
             lanes = slice(head * HEAD_SIZE, (head + 1) * HEAD_SIZE)
             key_total += dot(dscores[head, here, to], query_ref[here, lanes], tn)
             value_total += dot(
-                probs[head, here, to].astype(jnp.bfloat16),
+                probs_t[owner_chip, head, to],
                 accum[here, lanes].astype(jnp.bfloat16),
-                tn,
+                nn,
             )
         kv_grads[0, to] = key_total
         kv_grads[1, to] = value_total
+
+    def transpose_probs(owner_chip):
+        for head in range(heads):
+            probs_t[owner_chip, head] = probs[head, chip_rows(owner_chip)].T.astype(jnp.bfloat16)
+
+    def query_put(owner_chip):
+        here = chip_rows(owner_chip)
+        return pltpu.make_async_copy(
+            query_grad_ref.at[here], query_grad_out.at[here], out_sem.at[owner_chip]
+        )
 
     def query_part(owner_chip):
         here = chip_rows(owner_chip)
@@ -278,6 +294,7 @@
             query_grad_ref[here, lanes] = jnp.dot(
                 dscores[head, here], key_ref[...], preferred_element_type=jnp.float32
             ).astype(jnp.bfloat16)
+        query_put(owner_chip).start()
 
     def project(owner_chip, step):
         here = chip_rows(owner_chip)
@@ -364,6 +381,10 @@
     if last - 1 - lead > 0:
         step_with_weights(last - 1 - lead, False, False)
 
+    @pl.loop(0, chip_count)
+    def _(owner_chip):
+        transpose_probs(owner_chip)
+
     for step in range(last - lead, last):
         far_step(step)
         sum_step(step, False, False)
@@ -388,10 +409,12 @@
     for other in far_chips:
         kv_part(other, 1 - core)
     kv_copy.start()
+    sum_step(last, False, True)
+    weight_put.start()
+    for other in far_chips:
+        query_part(other)
     for other in far_chips:
         kv_part(other, core)
-        query_part(other)
-    sum_step(last, False, True)
     kv_copy.wait()
     mine = pl.ds(pl.multiple_of(core * half_rows, half_rows), half_rows)
     key_grad_ref[...] = (kv_grads[0, mine] + kv_in[0]).astype(jnp.bfloat16)
@@ -410,6 +433,12 @@
         for side in (0, 1):
             weight_copy(side, step).wait_send()
             sum_copy(side, step).wait_send()
+
+    weight_put.wait()
+
+    @pl.loop(0, chip_count)
+    def _(owner_chip):
+        query_put(owner_chip).wait()
 
     for side in (0, 1):
         weight_copy(side, 0).wait_send()
@@ -472,7 +501,7 @@
             anywhere,
             pl.BlockSpec(memory_space=pltpu.SMEM),
         ],
-        out_specs=(vmem, vmem, vmem, vmem),
+        out_specs=(anywhere, vmem, vmem, anywhere),
         scratch_shapes=[
             pltpu.VMEM((2, dp_count, seq_len, half), jnp.bfloat16),
             pltpu.VMEM((2, dp_count, depth, half), jnp.bfloat16),
@@ -482,7 +511,18 @@
             pltpu.VMEM((seq_len, depth), jnp.bfloat16),
             pltpu.VMEM((seq_len, HEAD_SIZE), jnp.bfloat16),
             pltpu.VMEM((seq_len, HEAD_SIZE), jnp.bfloat16),
+            pltpu.VMEM((seq_len, depth), jnp.bfloat16),
+            pltpu.VMEM((depth, width), jnp.float32),
             pltpu.VMEM((depth // HEAD_SIZE, seq_len, seq_len), jnp.float32),
+            pltpu.VMEM(
+                (
+                    tensor_count // 2,
+                    depth // HEAD_SIZE,
+                    seq_len,
+                    seq_len // (tensor_count // 2),
+                ),
+                jnp.bfloat16,
+            ),
             pltpu.VMEM((depth // HEAD_SIZE, seq_len, seq_len), jnp.bfloat16),
             pltpu.VMEM((seq_len, depth), jnp.bfloat16),
             pltpu.VMEM((depth, seq_len), jnp.bfloat16),
@@ -503,6 +543,7 @@
             dma,
             dma,
             dma((3,)),
+            dma((tensor_count // 2 + 1,)),
         ],
         compiler_params=pltpu.CompilerParams(
             collective_id=0, has_side_effects=True, vmem_limit_bytes=60 * 1024 * 1024

time: 108 us -> 107 us (level)
  no operation moved by 1% of the time
where the time goes in v4:
time: 107 us
  Pallas kernels  106 us (99%)
    pallas_call x1, Pallas kernels, shards(): pl.pallas_call(functools.partial(exchange_kernel, dp_count, tensor_count)...  104 us
    pallas_call x1, Pallas kernels, finish(): pl.pallas_call(finish_kernel, out_shape=tuple((jax.ShapeDtypeStruct(value...  2.51 us

profile of v4, /device:TPU:1, one launch (start us, length us, event | category | flops | bytes accessed | tf_op | source)
XLA Modules:
  0.0 107.2 jit_solution(17194162914088732736)
XLA Ops:
  0.6 103.9 %exchange.1 = (bf16[1024,256]{1,0:T(8,128)(2,1)}, bf16[512,128]{1,0:T(8,128)(2,1)}, bf16[512,128]{1,0:T(8,128)(2,1)}, f32[256,1024]{1,0:T(8,128)}) custom-call(bf16[256,8192]{1,0:T(8,128)(2,1)} %bitcast.7, bf16[256,1024]{1,0:T(8,128)(2,1)} %weight_ref.1, bf16[1024,256]{1,0:T(8,128)(2,1)} %bitcast.8, bf16[1024,256]{1,0:T(8,128)(2,1)} %bitcast.9, ...), custom_call_target="tpu_custom_call" | custom-call | tf_op jit(solution)/shard_map/exchange/pallas_call | solution.py:488
  104.5 2.5 %finish.1 = (bf16[1024,256]{1,0:T(8,128)(2,1)}, bf16[512,128]{1,0:T(8,128)(2,1)}, bf16[512,128]{1,0:T(8,128)(2,1)}, f32[256,1024]{1,0:T(8,128)}) custom-call(bf16[1024,256]{1,0:T(8,128)(2,1)} %get-tuple-element.12.refs_0_, bf16[512,128]{1,0:T(8,128)(2,1)} %get-tuple-element.13.refs_1_, bf16[512,128]{1,0:T(8,128)(2,1)} %get-tuple-element.14.refs_2_, ...), custom_call_target="tpu_custom_call" | custom-call | tf_op jit(solution)/shard_map/finish/pallas_call | solution.py:466
